TPU v7x, 32 devices: a whole 2x2x4 slice. The times are simulated.
32 devices in a mesh: row: 16 (over z, y, core), col: 2 (over x).
Axes of the slice: x: 2, y: 2, z: 4, core: 2. Of those that a mesh axis runs over, the one named last changes fastest.
Arguments:
- layer_input: bfloat16 [16384, 1152], P(('row', 'col')), may hold values from -6 to 6
- attn_gain: bfloat16 [1152], replicated, may hold values from 0.099609375 to 1.8984375
- mlp_gain: bfloat16 [1152], replicated, may hold values from 0.099609375 to 1.8984375
- query_weight: bfloat16 [1152, 1152], P('row', 'col'), may hold values from -0.1875 to 0.1875
- key_weight: bfloat16 [1152, 384], P('row', 'col'), may hold values from -0.1875 to 0.1875
- value_weight: bfloat16 [1152, 384], P('row', 'col'), may hold values from -0.1875 to 0.1875
- out_weight: bfloat16 [1152, 1152], P('col', 'row'), may hold values from -4 to 4
- gate_weight: bfloat16 [1152, 3072], P('row', 'col'), may hold values from -0.1875 to 0.1875
- up_weight: bfloat16 [1152, 3072], P('row', 'col'), may hold values from -0.1875 to 0.1875
- down_weight: bfloat16 [3072, 1152], P('col', 'row'), may hold values from -0.109375 to 0.109375
- seq_ids: int32 [16384], P('row'), may hold values from 0 to 31, as said below
- block_ends: int32 [16384], P('row'), may hold values from 255 to 16383, as said below
- grad_output: bfloat16 [16384, 1152], P(('row', 'col')), may hold values from -6 to 6
Outputs:
- layer_output: bfloat16 [16384, 1152], P(('row', 'col'))
- grad_input: bfloat16 [16384, 1152], P(('row', 'col'))
- grad_attn_gain: float32 [1152], replicated
- grad_mlp_gain: float32 [1152], replicated
- grad_query: float32 [1152, 1152], P('row', 'col')
- grad_key: float32 [1152, 384], P('row', 'col')
- grad_value: float32 [1152, 384], P('row', 'col')
- grad_out_weight: float32 [1152, 1152], P('col', 'row')
- grad_gate: float32 [1152, 3072], P('row', 'col')
- grad_up: float32 [1152, 3072], P('row', 'col')
- grad_down: float32 [3072, 1152], P('col', 'row')
Inputs may be any that keep to these rules, and one draw needn't show every extreme that they name: `seq_ids`: ids never fall; span number s of the aligned spans of 1024 tokens holds exactly two sequences, with ids 2 * s and 2 * s + 1, each of 256 tokens or more. `block_ends`: values never fall; an attention block is a run of 1 to 256 tokens inside one sequence, and the first block of every sequence has exactly 256 tokens.
All inputs are finite; a program needn't handle non-finite values.
Results may differ from a plain program's by a relative error of at most 0.014.
The roundings to bfloat16 on the way count: a program that leaves them out, or rounds other values in their place, can miss the bound.
Values may be sent and summed in bfloat16 or wider, within the bound.
A program may use at most 192 MiB of HBM per device.

v0:
```python
import math
import jax
import jax.numpy as jnp
from jax import lax
from jax.sharding import PartitionSpec as P

QUERY_HEADS = 18
KEY_VALUE_HEADS = 6
HEAD_SIZE_DIM = 64
eps = 1e-05
rope_base = 10000.0
neg_fill = -1e30


def rotate_half(values, head_size):
    lane_index = jnp.arange(values.shape[-1], dtype=jnp.int32) % head_size
    forward_roll = jnp.roll(values, -(head_size // 2), axis=-1)
    backward_roll = jnp.roll(values, head_size // 2, axis=-1)
    return jnp.where(lane_index < head_size // 2, -forward_roll, backward_roll)


def rope_tables(position, table_width, head_size):
    lane_index = (jnp.arange(table_width, dtype=jnp.int32) % (head_size // 2)).astype(jnp.float32)
    frequency = jnp.exp(lane_index * (-2.0 * math.log(rope_base) / head_size))
    angles = position[:, None] * frequency[None, :]
    return (jnp.cos(angles), jnp.sin(angles))


def rotary(values, cosine, sine_part, head_size):
    return values * cosine + rotate_half(values, head_size) * sine_part


def rotary_back(upstream, cosine, sine_part, head_size):
    return upstream * cosine - rotate_half(upstream * sine_part, head_size)


def positions(seq_ids):
    token_index = jnp.arange(seq_ids.shape[0], dtype=jnp.int32)
    earlier = jnp.concatenate([seq_ids[:1] - 1, seq_ids[:-1]])
    seq_start = lax.cummax(jnp.where(seq_ids != earlier, token_index, 0), axis=0)
    return (token_index - seq_start).astype(jnp.float32)


def visible(query_seq, query_end, seq_ids, block_ends):
    return (query_seq[:, None] == seq_ids[None, :]) & (block_ends[None, :] <= query_end[:, None])


def to_rows(values):
    return lax.all_to_all(values, "col", split_axis=0, concat_axis=1, tiled=True)


def to_tokens(values):
    return lax.all_to_all(values, "col", split_axis=1, concat_axis=0, tiled=True)


def col_sums(values):
    return lax.psum_scatter(values, "col", scatter_dimension=0, tiled=True)


def widen(values):
    return lax.all_gather(values, "col", axis=0, tiled=True)


def shards(
    layer_input,
    attn_gain,
    mlp_gain,
    query_weight,
    key_weight,
    value_weight,
    out_weight,
    gate_weight,
    up_weight,
    down_weight,
    seq_ids,
    block_ends,
    grad_output,
):
    col_index = lax.axis_index("col")
    query_rows = layer_input.shape[0]
    block_rows = min(512, query_rows)
    block_count = query_rows // block_rows
    heads_per_group = QUERY_HEADS // KEY_VALUE_HEADS
    group_head_width = heads_per_group * HEAD_SIZE_DIM
    query_width = QUERY_HEADS * HEAD_SIZE_DIM
    score_scale = HEAD_SIZE_DIM ** (-0.5)
    attn_gain_float = attn_gain.astype(jnp.float32)
    mlp_gain_float = mlp_gain.astype(jnp.float32)
    full_input = lax.all_gather(layer_input, "col", axis=0, tiled=True)
    token_rows = full_input.shape[0]
    query_cols, key_cols, value_cols, out_rows, gate_cols, up_cols, down_rows = (
        lax.all_gather(query_weight, "row", axis=0, tiled=True),
        lax.all_gather(key_weight, "row", axis=0, tiled=True),
        lax.all_gather(value_weight, "row", axis=0, tiled=True),
        lax.all_gather(out_weight, "row", axis=1, tiled=True),
        lax.all_gather(gate_weight, "row", axis=0, tiled=True),
        lax.all_gather(up_weight, "row", axis=0, tiled=True),
        lax.all_gather(down_weight, "row", axis=1, tiled=True),
    )
    input_float = full_input.astype(jnp.float32)
    inv_all = lax.rsqrt(jnp.mean(input_float * input_float, axis=1, keepdims=True) + eps)
    attn_in = (input_float * inv_all * attn_gain_float).astype(jnp.bfloat16)
    query_unrotated = jnp.dot(attn_in, query_cols, preferred_element_type=jnp.float32).astype(
        jnp.bfloat16
    )
    key_raw = jnp.dot(attn_in, key_cols, preferred_element_type=jnp.float32).astype(jnp.bfloat16)
    value_projected = jnp.dot(attn_in, value_cols, preferred_element_type=jnp.float32).astype(
        jnp.bfloat16
    )
    query_all = to_rows(query_unrotated)
    key_all, value_all = (
        lax.all_gather(key_raw, "col", axis=1, tiled=True),
        lax.all_gather(value_projected, "col", axis=1, tiled=True),
    )
    position = positions(seq_ids)
    row_start = col_index * query_rows
    query_pos = lax.dynamic_slice_in_dim(position, row_start, query_rows)
    query_seq = lax.dynamic_slice_in_dim(seq_ids, row_start, query_rows)
    query_end = lax.dynamic_slice_in_dim(block_ends, row_start, query_rows)
    query_cos, query_sin = rope_tables(query_pos, query_width, HEAD_SIZE_DIM)
    key_cos, key_sin = rope_tables(position, key_all.shape[1], HEAD_SIZE_DIM)
    query_rotated = (
        rotary(query_all.astype(jnp.float32), query_cos, query_sin, HEAD_SIZE_DIM) * score_scale
    ).astype(jnp.bfloat16)
    key_rotated = rotary(key_all.astype(jnp.float32), key_cos, key_sin, HEAD_SIZE_DIM).astype(
        jnp.bfloat16
    )

    def block_inputs(block_index):
        first_row = block_index * block_rows
        allowed = visible(query_seq, query_end, seq_ids, block_ends)
        return (first_row, allowed)

    def group_scores(query_block, group_index, allowed):
        query_head_rows = lax.dynamic_slice_in_dim(
            query_block, group_index * group_head_width, group_head_width, 1
        ).reshape(block_rows, heads_per_group, HEAD_SIZE_DIM)
        key_group = lax.dynamic_slice_in_dim(
            key_rotated, group_index * HEAD_SIZE_DIM, HEAD_SIZE_DIM, 1
        )
        value_group = lax.dynamic_slice_in_dim(
            value_all, group_index * HEAD_SIZE_DIM, HEAD_SIZE_DIM, 1
        )
        scores = jnp.einsum(
            "qhd,kd->hqk", query_head_rows, key_group, preferred_element_type=jnp.float32
        )
        return (query_head_rows, key_group, value_group, jnp.where(allowed[None], scores, neg_fill))

    def attend_block(block_index):
        first_row, allowed = block_inputs(block_index)

        def attend_head_group(group_index):
            query_head_rows, key_group, value_group, scores = group_scores(
                query_rotated, group_index, allowed
            )
            row_top = jnp.max(scores, axis=2, keepdims=True)
            powers = jnp.exp(scores - row_top)
            exp_total = jnp.sum(powers, axis=2, keepdims=True)
            attn_probs = (powers / exp_total).astype(jnp.bfloat16)
            weighted_values = jnp.einsum(
                "hqk,kd->qhd", attn_probs, value_group, preferred_element_type=jnp.float32
            )
            return (
                weighted_values.reshape(block_rows, group_head_width),
                (row_top + jnp.log(exp_total))[:, :, 0],
            )

        weighted_value_rows, logsumexp_rows = lax.map(
            attend_head_group, jnp.arange(KEY_VALUE_HEADS, dtype=jnp.int32)
        )
        return (
            jnp.transpose(weighted_value_rows, (1, 0, 2)).reshape(block_rows, query_width),
            logsumexp_rows,
        )

    mixed_blocks, log_blocks = lax.map(attend_block, jnp.arange(block_count, dtype=jnp.int32))
    attn_rows = mixed_blocks.reshape(query_rows, query_width).astype(jnp.bfloat16)
    attn_tokens = to_tokens(attn_rows)
    attn_share = col_sums(jnp.dot(attn_tokens, out_rows, preferred_element_type=jnp.float32))
    residual = layer_input.astype(jnp.float32) + attn_share
    inv_two = lax.rsqrt(jnp.mean(residual * residual, axis=1, keepdims=True) + eps)
    normed_two = residual * inv_two
    mlp_in = widen((normed_two * mlp_gain_float).astype(jnp.bfloat16))
    gate_act = jnp.dot(mlp_in, gate_cols, preferred_element_type=jnp.float32)
    up_act = jnp.dot(mlp_in, up_cols, preferred_element_type=jnp.float32)
    hidden = (jax.nn.silu(gate_act) * up_act).astype(jnp.bfloat16)
    mlp_share = col_sums(jnp.dot(hidden, down_rows, preferred_element_type=jnp.float32))
    layer_output = (residual + mlp_share).astype(jnp.bfloat16)
    grad_float = grad_output.astype(jnp.float32)
    grad_full = widen(grad_output)
    grad_down = jnp.einsum("tf,td->fd", hidden, grad_full, preferred_element_type=jnp.float32)
    grad_hidden = jnp.einsum("td,fd->tf", grad_full, down_rows, preferred_element_type=jnp.float32)
    gate_sigmoid = jax.nn.sigmoid(gate_act)
    grad_gate_act = (
        grad_hidden * up_act * gate_sigmoid * (1.0 + gate_act * (1.0 - gate_sigmoid))
    ).astype(jnp.bfloat16)
    grad_up_act = (grad_hidden * gate_act * gate_sigmoid).astype(jnp.bfloat16)
    grad_gate = jnp.einsum("td,tf->df", mlp_in, grad_gate_act, preferred_element_type=jnp.float32)
    grad_up = jnp.einsum("td,tf->df", mlp_in, grad_up_act, preferred_element_type=jnp.float32)
    grad_mlp_share = col_sums(
        jnp.einsum("tf,df->td", grad_gate_act, gate_cols, preferred_element_type=jnp.float32)
        + jnp.einsum("tf,df->td", grad_up_act, up_cols, preferred_element_type=jnp.float32)
    )
    scaled_two = grad_mlp_share * mlp_gain_float
    inner_two = jnp.mean(scaled_two * normed_two, axis=1, keepdims=True)
    grad_residual = grad_float + inv_two * (scaled_two - normed_two * inner_two)
    grad_mlp_gain = jnp.sum(grad_mlp_share * normed_two, axis=0)
    grad_branch = grad_residual.astype(jnp.bfloat16)
    grad_attn_full = widen(grad_branch)
    grad_out_weight = jnp.einsum(
        "tq,td->qd", attn_tokens, grad_attn_full, preferred_element_type=jnp.float32
    )
    grad_mixture = to_rows(
        jnp.einsum(
            "td,qd->tq", grad_attn_full, out_rows, preferred_element_type=jnp.float32
        ).astype(jnp.bfloat16)
    )

    def back_block(carried_state, scan_items):
        block_index, block_log_total = scan_items
        first_row, allowed = block_inputs(block_index)

        def backward_head_group(inner_acc, group_items):
            group_index, log_group = group_items
            keys_acc, values_acc = inner_acc
            query_head_rows, key_group, value_group, scores = group_scores(
                query_rotated, group_index, allowed
            )
            attn_probs = jnp.exp(scores - log_group[:, :, None])
            grad_heads = lax.dynamic_slice_in_dim(
                grad_mixture, group_index * group_head_width, group_head_width, 1
            ).reshape(block_rows, heads_per_group, HEAD_SIZE_DIM)
            grad_probs = jnp.einsum(
                "qhd,kd->hqk", grad_heads, value_group, preferred_element_type=jnp.float32
            )
            value_piece = jnp.einsum(
                "hqk,qhd->kd",
                attn_probs.astype(jnp.bfloat16),
                grad_heads,
                preferred_element_type=jnp.float32,
            )
            inner_dot = jnp.sum(attn_probs * grad_probs, axis=2, keepdims=True)
            grad_scores = (attn_probs * (grad_probs - inner_dot)).astype(jnp.bfloat16)
            query_piece = jnp.einsum(
                "hqk,kd->qhd", grad_scores, key_group, preferred_element_type=jnp.float32
            ).reshape(block_rows, group_head_width)
            key_piece = jnp.einsum(
                "hqk,qhd->kd", grad_scores, query_head_rows, preferred_element_type=jnp.float32
            )
            column = group_index * HEAD_SIZE_DIM
            keys_acc = lax.dynamic_update_slice_in_dim(
                keys_acc,
                lax.dynamic_slice_in_dim(keys_acc, column, HEAD_SIZE_DIM, 1) + key_piece,
                column,
                1,
            )
            values_acc = lax.dynamic_update_slice_in_dim(
                values_acc,
                lax.dynamic_slice_in_dim(values_acc, column, HEAD_SIZE_DIM, 1) + value_piece,
                column,
                1,
            )
            return ((keys_acc, values_acc), query_piece)

        carried_state, query_pieces = lax.scan(
            backward_head_group,
            carried_state,
            (jnp.arange(KEY_VALUE_HEADS, dtype=jnp.int32), block_log_total),
        )
        return (
            carried_state,
            jnp.transpose(query_pieces, (1, 0, 2)).reshape(block_rows, query_width),
        )

    zeros_kv = jnp.zeros((token_rows, key_all.shape[1]), jnp.float32)
    (grad_keys, grad_values), query_blocks = lax.scan(
        back_block, (zeros_kv, zeros_kv), (jnp.arange(block_count, dtype=jnp.int32), log_blocks)
    )
    grad_query_rot = query_blocks.reshape(query_rows, query_width)
    grad_query_raw = to_tokens(
        rotary_back(grad_query_rot * score_scale, query_cos, query_sin, HEAD_SIZE_DIM).astype(
            jnp.bfloat16
        )
    )
    grad_key_part = rotary_back(grad_keys, key_cos, key_sin, HEAD_SIZE_DIM)
    grad_key_sum, grad_value_sum = (
        lax.psum_scatter(grad_key_part, "col", scatter_dimension=1, tiled=True),
        lax.psum_scatter(grad_values, "col", scatter_dimension=1, tiled=True),
    )
    grad_key_raw = grad_key_sum.astype(jnp.bfloat16)
    grad_value_raw = grad_value_sum.astype(jnp.bfloat16)
    grad_query = jnp.einsum(
        "td,tq->dq", attn_in, grad_query_raw, preferred_element_type=jnp.float32
    )
    grad_key = jnp.einsum("td,tq->dq", attn_in, grad_key_raw, preferred_element_type=jnp.float32)
    grad_value = jnp.einsum(
        "td,tq->dq", attn_in, grad_value_raw, preferred_element_type=jnp.float32
    )
    grad_attn_share = col_sums(
        jnp.einsum("tq,dq->td", grad_query_raw, query_cols, preferred_element_type=jnp.float32)
        + jnp.einsum("tq,dq->td", grad_key_raw, key_cols, preferred_element_type=jnp.float32)
        + jnp.einsum("tq,dq->td", grad_value_raw, value_cols, preferred_element_type=jnp.float32)
    )
    own_float = layer_input.astype(jnp.float32)
    inv_one = lax.rsqrt(jnp.mean(own_float * own_float, axis=1, keepdims=True) + eps)
    normed_one = own_float * inv_one
    scaled_one = grad_attn_share * attn_gain_float
    inner_one = jnp.mean(scaled_one * normed_one, axis=1, keepdims=True)
    grad_input = (grad_residual + inv_one * (scaled_one - normed_one * inner_one)).astype(
        jnp.bfloat16
    )
    grad_attn_gain = jnp.sum(grad_attn_share * normed_one, axis=0)
    weight_sums = (
        lax.psum_scatter(grad_query, "row", scatter_dimension=0, tiled=True),
        lax.psum_scatter(grad_key, "row", scatter_dimension=0, tiled=True),
        lax.psum_scatter(grad_value, "row", scatter_dimension=0, tiled=True),
        lax.psum_scatter(grad_out_weight, "row", scatter_dimension=1, tiled=True),
        lax.psum_scatter(grad_gate, "row", scatter_dimension=0, tiled=True),
        lax.psum_scatter(grad_up, "row", scatter_dimension=0, tiled=True),
        lax.psum_scatter(grad_down, "row", scatter_dimension=1, tiled=True),
    )
    gain_sums = lax.psum((grad_attn_gain, grad_mlp_gain), ("row", "col"))
    return (
        layer_output,
        grad_input,
        gain_sums[0],
        gain_sums[1],
        weight_sums[0],
        weight_sums[1],
        weight_sums[2],
        weight_sums[3],
        weight_sums[4],
        weight_sums[5],
        weight_sums[6],
    )


def solution(mesh):
    in_specs = (
        P(("row", "col"), None),
        P(),
        P(),
        P("row", "col"),
        P("row", "col"),
        P("row", "col"),
        P("col", "row"),
        P("row", "col"),
        P("row", "col"),
        P("col", "row"),
        P("row"),
        P("row"),
        P(("row", "col"), None),
    )
    out_specs = (
        P(("row", "col"), None),
        P(("row", "col"), None),
        P(),
        P(),
        P("row", "col"),
        P("row", "col"),
        P("row", "col"),
        P("col", "row"),
        P("row", "col"),
        P("row", "col"),
        P("col", "row"),
    )
    return jax.shard_map(shards, mesh=mesh, in_specs=in_specs, out_specs=out_specs, check_vma=False)
```

profile of v0, /device:TPU:0, one launch (start us, length us, event | category | flops | bytes accessed | tf_op | source)
XLA Modules:
  0.0 1523.2 jit_solution(14034235379282888117)
XLA Ops:
  14.5 24.8 %all_gather.42 = bf16[1152,192]{1,0:T(8,128)(2,1)S(1)} all-gather(bf16[72,192]{1,0:T(8,128)(2,1)S(1)} %copy-done.33), channel_id=1, replica_groups=mesh['row'=16,'col'=2] {'row'}, dimensions={0}, use_global_device_ids=true | all-gather | bytes 470016 | tf_op jit(solution)/shard_map/all_gather | solution.py:93
  39.4 19.0 %all_gather.40 = bf16[1152,192]{1,0:T(8,128)(2,1)S(1)} all-gather(bf16[72,192]{1,0:T(8,128)(2,1)S(1)} %copy-done.34), channel_id=1, replica_groups=mesh['row'=16,'col'=2] {'row'}, dimensions={0}, use_global_device_ids=true | all-gather | bytes 470016 | tf_op jit(solution)/shard_map/all_gather | solution.py:94
  62.2 12.0 all_gather.43
  76.2 11.4 all_gather.41
  115.5 11.3 fusion.64
  126.8 62.2 %while.50 = (s32[]{:T(128)}, bf16[6,512,192]{1,2,0:T(8,128)(2,1)S(1)}, f32[6,3,512]{2,1,0:T(4,128)}, s32[6]{0:T(128)S(1)}, bf16[1024,384]{0,1:T(8,128)(2,1)}, /*...) while((s32[]{:T(128)}, ...), condition=%wide.region_6.7_spmd.clone.clone, body=%wide.region_3.6_spmd.clone.sunk.clone | while | flops 418380288 | bytes 22477056 | solution.py:168
  189.0 17.3 %all_to_all.64 = bf16[512,2,576]{0,2,1:T(8,128)(2,1)S(1)} all-to-all(bf16[512,2,576]{0,2,1:T(8,128)(2,1)S(1)} %bitcast.276), channel_id=1, replica_groups=mesh['row'=16,'col'=2] {'col'}, dimensions={1} | all-to-all | bytes 2359296 | tf_op jit(solution)/shard_map/all_to_all | solution.py:53
  214.1 56.8 %reduce-scatter.18.cloned.1.call-done = f32[512,1152]{1,0:T(8,128)} async-done(((f32[1024,1152]{1,0:T(8,128)}), f32[512,1152]{1,0:T(8,128)}) %reduce-scatter.18.cloned.1.call-update) | async-done | bytes 2359312 | tf_op jit(solution)/shard_map/reduce_scatter | solution.py:57
  277.9 42.6 %all-gather.20.cloned.1.call-done = bf16[1152,1536]{1,0:T(8,128)(2,1)} async-done(((bf16[72,1536]{1,0:T(8,128)(2,1)}), bf16[1152,1536]{1,0:T(8,128)(2,1)}) %all-gather.20.cloned.1.call-update) | async-done | bytes 3538960 | tf_op jit(solution)/shard_map/all_gather | solution.py:97
  320.5 37.1 %all-gather.16.cloned.1.call-done = bf16[1024,1152]{1,0:T(8,128)(2,1)} async-done(((bf16[512,1152]{1,0:T(8,128)(2,1)}), bf16[1024,1152]{1,0:T(8,128)(2,1)}) %all-gather.16.cloned.1.call-update) | async-done | bytes 2359312 | tf_op jit(solution)/shard_map/all_gather | solution.py:61
  357.6 9.6 fusion.126
  367.3 40.2 %all-gather.18.cloned.1.call-done = bf16[1152,1536]{1,0:T(8,128)(2,1)} async-done(((bf16[72,1536]{1,0:T(8,128)(2,1)}), bf16[1152,1536]{1,0:T(8,128)(2,1)}) %all-gather.18.cloned.1.call-update) | async-done | bytes 3538960 | tf_op jit(solution)/shard_map/all_gather | solution.py:96
  407.4 9.7 fusion.125
  417.1 27.0 %all-gather.24.cloned.1.call-done = bf16[1024,1152]{1,0:T(8,128)(2,1)} async-done(((bf16[512,1152]{1,0:T(8,128)(2,1)}), bf16[1024,1152]{1,0:T(8,128)(2,1)}) %all-gather.24.cloned.1.call-update) | async-done | bytes 2359312 | tf_op jit(solution)/shard_map/all_gather | solution.py:61
  444.1 49.8 %all-gather.22.cloned.1.call-done = bf16[1536,1152]{0,1:T(8,128)(2,1)} async-done(((bf16[1536,72]{0,1:T(8,128)(2,1)}), bf16[1536,1152]{0,1:T(8,128)(2,1)}) %all-gather.22.cloned.1.call-update) | async-done | bytes 3538960 | tf_op jit(solution)/shard_map/all_gather | solution.py:98
  493.9 12.5 multiply_convert_fusion
  516.8 59.1 %reduce-scatter.22.cloned.1.call-done = f32[512,1152]{1,0:T(8,128)} async-done(((f32[1024,1152]{1,0:T(8,128)}), f32[512,1152]{1,0:T(8,128)}) %reduce-scatter.22.cloned.1.call-update) | async-done | bytes 2359312 | tf_op jit(solution)/shard_map/reduce_scatter | solution.py:57
  581.8 36.2 %all-gather.26.cloned.1.call-done = bf16[1024,1152]{1,0:T(8,128)(2,1)} async-done(((bf16[512,1152]{1,0:T(8,128)(2,1)}), bf16[1024,1152]{1,0:T(8,128)(2,1)}) %all-gather.26.cloned.1.call-update) | async-done | bytes 2359312 | tf_op jit(solution)/shard_map/all_gather | solution.py:61
  627.7 15.1 all-to-all-done.2
  645.5 125.0 %while.51 = (s32[]{:T(128)}, f32[1024,384]{0,1:T(8,128)}, f32[1024,384]{0,1:T(8,128)}, f32[6,512,192]{1,2,0:T(8,128)}, s32[6]{0:T(128)S(1)}, /*index=5*/bf16[102...) while((s32[]{:T(128)}, f32[1024,384]{0,1:T(8,128)}, ...), condition=%wide.region_15.16_spmd.clone.clone, body=%wide.region_13.15_spmd.clone.sunk.clone | while | flops 1027209728 | bytes 55630144 | solution.py:265
  796.7 8.7 subtract_convert_fusion
  805.4 18.5 %all_to_all.65 = bf16[512,2,576]{0,2,1:T(8,128)(2,1)S(1)} all-to-all(bf16[512,2,576]{0,2,1:T(8,128)(2,1)S(1)} %subtract_convert_fusion), channel_id=1, replica_groups=mesh['row'=16,'col'=2] {'col'}, dimensions={1} | all-to-all | bytes 2359296 | tf_op jit(solution)/shard_map/all_to_all | solution.py:53
  846.7 9.4 fusion.127
  909.8 40.1 %all-reduce.2 = (f32[1152]{0:T(1024)}, f32[1152]{0:T(1024)}) all-reduce(f32[1152]{0:T(1024)} %get-tuple-element.251, f32[1152]{0:T(1024)} %get-tuple-element.249), channel_id=1, replica_groups=mesh['row'=16,'col'=2] {'row','col'}, use_global_device_ids=true, to_apply=%region_21.22 | all-reduce | flops 2304 | bytes 18432 | tf_op jit(solution)/shard_map/psum | solution.py:322
  951.1 19.2 %reduce-scatter.20.cloned.1.call-done = f32[512,1152]{1,0:T(8,128)} async-done(((f32[1024,1152]{1,0:T(8,128)}), f32[512,1152]{1,0:T(8,128)}) %reduce-scatter.20.cloned.1.call-update) | async-done | bytes 2359312 | tf_op jit(solution)/shard_map/reduce_scatter | solution.py:57
  975.4 89.2 %reduce-scatter.38.cloned.1.call-done = f32[1536,72]{0,1:T(8,128)} async-done(((f32[1536,1152]{0,1:T(8,128)}), f32[1536,72]{0,1:T(8,128)}) %reduce-scatter.38.cloned.1.call-update) | async-done | bytes 442384 | tf_op jit(solution)/shard_map/reduce_scatter | solution.py:320
  1064.7 94.5 %reduce-scatter.36.cloned.1.call-done = f32[72,1536]{1,0:T(8,128)} async-done(((f32[1152,1536]{1,0:T(8,128)}), f32[72,1536]{1,0:T(8,128)}) %reduce-scatter.36.cloned.1.call-update) | async-done | bytes 442384 | tf_op jit(solution)/shard_map/reduce_scatter | solution.py:319
  1159.2 94.0 %reduce-scatter.34.cloned.1.call-done = f32[72,1536]{1,0:T(8,128)} async-done(((f32[1152,1536]{1,0:T(8,128)}), f32[72,1536]{1,0:T(8,128)}) %reduce-scatter.34.cloned.1.call-update) | async-done | bytes 442384 | tf_op jit(solution)/shard_map/reduce_scatter | solution.py:318
  1253.3 69.9 %reduce-scatter.42.cloned.1.call-done = f32[576,72]{0,1:T(8,128)} async-done(((f32[576,1152]{0,1:T(8,128)}), f32[576,72]{0,1:T(8,128)}) %reduce-scatter.42.cloned.1.call-update) | async-done | bytes 165904
  1323.1 61.6 %reduce-scatter.32.cloned.1.call-done = f32[72,192]{1,0:T(8,128)} async-done(((f32[1152,192]{1,0:T(8,128)}), f32[72,192]{1,0:T(8,128)}) %reduce-scatter.32.cloned.1.call-update) | async-done | bytes 55312 | tf_op jit(solution)/shard_map/reduce_scatter | solution.py:316
  1384.8 61.8 %reduce-scatter.30.cloned.1.call-done = f32[72,192]{1,0:T(8,128)} async-done(((f32[1152,192]{1,0:T(8,128)}), f32[72,192]{1,0:T(8,128)}) %reduce-scatter.30.cloned.1.call-update) | async-done | bytes 55312 | tf_op jit(solution)/shard_map/reduce_scatter | solution.py:315
  1446.6 69.3 %reduce-scatter.40.cloned.1.call-done = f32[72,576]{1,0:T(8,128)} async-done(((f32[1152,576]{1,0:T(8,128)}), f32[72,576]{1,0:T(8,128)}) %reduce-scatter.40.cloned.1.call-update) | async-done | bytes 165904
  (358 shorter events, 363.0 us)
Async XLA Ops:
  7.2 51.2 %all-gather.10.cloned.1.call-start = ((), (), s32[]{:S(2)}) async-start(), calls=%async_computation.17 | async-start | bytes 3538944 | tf_op jit(solution)/shard_map/all_gather | solution.py:89
  8.0 82.0 %all-gather.12.cloned.1.call-start = ((), (), s32[]{:S(2)}) async-start(), calls=%async_computation.18 | async-start | bytes 1566720 | tf_op jit(solution)/shard_map/all_gather | solution.py:92
  8.7 197.8 %all-gather.14.cloned.1.call-start = ((), (), s32[]{:S(2)}) async-start(), calls=%async_computation.19 | async-start | bytes 1566720 | tf_op jit(solution)/shard_map/all_gather | solution.py:95
  13.9 47.0 %copy-start.24 = (f32[1024]{0:T(1024)}, f32[1024]{0:T(1024)S(1)}, u32[]{:S(2)}) copy-start(f32[1024]{0:T(1024)S(1)} %fusion.97) | copy-start | bytes 12292
  95.1 19.3 %all-to-all-start = ((bf16[2,512,576]{1,2,0:T(8,128)(2,1)}), bf16[2,512,576]{1,2,0:T(8,128)(2,1)S(1)}, u32[]{:S(2)}, u32[]{:S(2)}) async-start(bf16[2,512,576]{1,2,0:T(8,128)(2,1)} %bitcast.277), calls=%async_computation | async-start | bytes 2359296 | tf_op jit(solution)/shard_map/all_to_all | solution.py:49
  98.7 172.2 %reduce-scatter.18.cloned.1.call-start = ((), (), s32[]{:S(2)}) async-start(), calls=%async_computation.20 | async-start | bytes 7077888 | tf_op jit(solution)/shard_map/reduce_scatter | solution.py:57
  212.8 58.1 %copy-start.7 = (bf16[512,1152]{1,0:T(8,128)(2,1)S(1)}, bf16[512,1152]{1,0:T(8,128)(2,1)}, u32[]{:S(2)}) copy-start(bf16[512,1152]{1,0:T(8,128)(2,1)} %param.17) | copy-start | bytes 3538948
  212.8 107.7 %all-gather.20.cloned.1.call-start = ((), (), s32[]{:S(2)}) async-start(), calls=%async_computation.23 | async-start | bytes 3760128 | tf_op jit(solution)/shard_map/all_gather | solution.py:97
  213.4 144.2 %all-gather.16.cloned.1.call-start = ((), (), s32[]{:S(2)}) async-start(), calls=%async_computation.21 | async-start | bytes 3538944 | tf_op jit(solution)/shard_map/all_gather | solution.py:61
  273.7 305.2 %copy-start.1 = (f32[512,1152]{1,0:T(8,128)}, f32[512,1152]{1,0:T(8,128)S(1)}, u32[]{:S(2)}) copy-start(f32[512,1152]{1,0:T(8,128)S(1)} %get-tuple-element.306) | copy-start | bytes 7077892
  275.3 132.2 %all-gather.18.cloned.1.call-start = ((), (), s32[]{:S(2)}) async-start(), calls=%async_computation.22 | async-start | bytes 3760128 | tf_op jit(solution)/shard_map/all_gather | solution.py:96
  276.0 168.1 %all-gather.24.cloned.1.call-start = ((), (), s32[]{:S(2)}) async-start(), calls=%async_computation.26 | async-start | bytes 3538944 | tf_op jit(solution)/shard_map/all_gather | solution.py:61
  276.8 217.1 %all-gather.22.cloned.1.call-start = ((), (), s32[]{:S(2)}) async-start(), calls=%async_computation.24 | async-start | bytes 3760128 | tf_op jit(solution)/shard_map/all_gather | solution.py:98
  277.5 298.4 %reduce-scatter.22.cloned.1.call-start = ((), (), s32[]{:S(2)}) async-start(), calls=%async_computation.27 | async-start | bytes 7077888 | tf_op jit(solution)/shard_map/reduce_scatter | solution.py:57
  516.7 62.8 %copy-start.9 = (bf16[512,1152]{1,0:T(8,128)(2,1)S(1)}, bf16[512,1152]{1,0:T(8,128)(2,1)}, u32[]{:S(2)}) copy-start(bf16[512,1152]{1,0:T(8,128)(2,1)} %param.29) | copy-start | bytes 3538948
  516.7 101.3 %all-gather.26.cloned.1.call-start = ((), (), s32[]{:S(2)}) async-start(), calls=%async_computation.28 | async-start | bytes 3538944 | tf_op jit(solution)/shard_map/all_gather | solution.py:61
  623.0 19.8 %all-to-all-start.2 = ((bf16[2,512,576]{1,2,0:T(8,128)(2,1)}), bf16[2,512,576]{1,2,0:T(8,128)(2,1)}, u32[]{:S(2)}, u32[]{:S(2)}) async-start(bf16[2,512,576]{1,2,0:T(8,128)(2,1)} %bitcast.162), calls=%async_computation.5 | async-start | bytes 2359296 | tf_op jit(solution)/shard_map/all_to_all | solution.py:49
  627.4 201.0 %reduce-scatter.24.cloned.1.call-start = ((), (), s32[]{:S(2)}) async-start(), calls=%async_computation.29 | async-start | bytes 2359296 | tf_op jit(solution)/shard_map/reduce_scatter | solution.py:287
  645.5 125.0 %copy-start.26 = (f32[1024]{0:T(1024)S(1)}, f32[1024]{0:T(1024)}, u32[]{:S(2)}) copy-start(f32[1024]{0:T(1024)} %copy-done.24) | copy-start | bytes 12292
  645.5 125.0 %copy-start.36 = (f32[384]{0:T(512)S(1)}, f32[384]{0:T(512)}, u32[]{:S(2)}) copy-start(f32[384]{0:T(512)} %fusion.100) | copy-start | bytes 4612
  785.3 55.7 %reduce-scatter.26.cloned.1.call-start = ((), (), s32[]{:S(2)}) async-start(), calls=%async_computation.30 | async-start | bytes 2359296 | tf_op jit(solution)/shard_map/reduce_scatter | solution.py:288
  794.4 112.4 %reduce-scatter.28.cloned.1.call-start = ((), (), s32[]{:S(2)}) async-start(), calls=%async_computation.31 | async-start | bytes 7077888 | tf_op jit(solution)/shard_map/reduce_scatter | solution.py:57
  846.7 123.7 %reduce-scatter.20.cloned.1.call-start = ((), (), s32[]{:S(2)}) async-start(), calls=%async_computation.25 | async-start | bytes 7077888 | tf_op jit(solution)/shard_map/reduce_scatter | solution.py:57
  856.1 208.6 %reduce-scatter.38.cloned.1.call-start = ((), (), s32[]{:S(2)}) async-start(), calls=%async_computation.36 | async-start | bytes 7520256 | tf_op jit(solution)/shard_map/reduce_scatter | solution.py:320
  865.4 293.8 %reduce-scatter.36.cloned.1.call-start = ((), (), s32[]{:S(2)}) async-start(), calls=%async_computation.35 | async-start | bytes 7520256 | tf_op jit(solution)/shard_map/reduce_scatter | solution.py:319
  874.7 378.6 %reduce-scatter.34.cloned.1.call-start = ((), (), s32[]{:S(2)}) async-start(), calls=%async_computation.34 | async-start | bytes 7520256 | tf_op jit(solution)/shard_map/reduce_scatter | solution.py:318
  882.6 440.5 %reduce-scatter.42.cloned.1.call-start = ((), (), s32[]{:S(2)}) async-start(), calls=%async_computation.38 | async-start | bytes 3133440
  889.3 495.4 %reduce-scatter.32.cloned.1.call-start = ((), (), s32[]{:S(2)}) async-start(), calls=%async_computation.33 | async-start | bytes 1253376 | tf_op jit(solution)/shard_map/reduce_scatter | solution.py:316
  894.2 552.4 %reduce-scatter.30.cloned.1.call-start = ((), (), s32[]{:S(2)}) async-start(), calls=%async_computation.32 | async-start | bytes 1253376 | tf_op jit(solution)/shard_map/reduce_scatter | solution.py:315
  897.5 618.4 %reduce-scatter.40.cloned.1.call-start = ((), (), s32[]{:S(2)}) async-start(), calls=%async_computation.37 | async-start | bytes 3133440
  901.6 68.7 %copy-start.2 = (f32[512,1152]{1,0:T(8,128)S(1)}, f32[512,1152]{1,0:T(8,128)}, u32[]{:S(2)}) copy-start(f32[512,1152]{1,0:T(8,128)} %copy-done.1) | copy-start | bytes 7077892
  901.6 68.7 %copy-start.23 = (f32[1152]{0:T(1024)S(1)}, f32[1152]{0:T(1024)}, u32[]{:S(2)}) copy-start(f32[1152]{0:T(1024)} %convert_element_type.142) | copy-start | bytes 13828
  (51 other events, 326.2 us)
Sparse Core Ops, SparseCore 0:
  9.6 38.7 all-gather.9
  50.6 39.3 all-gather.11
  92.1 38.1 all-gather.13
  212.9 57.8 reduce-scatter.17
  273.3 47.1 all-gather.19
  322.5 35.0 all-gather.15
  360.2 47.1 all-gather.17
  409.0 35.0 all-gather.23
  446.7 47.1 all-gather.21
  516.8 58.9 reduce-scatter.21
  582.0 36.0 all-gather.25
  785.4 26.4 reduce-scatter.23
  814.2 26.7 reduce-scatter.25
  846.8 59.9 reduce-scatter.27
  909.1 61.2 reduce-scatter.19
  974.8 89.8 reduce-scatter.37
  1069.6 89.5 reduce-scatter.35
  1163.7 89.5 reduce-scatter.33
  1258.3 64.8 reduce-scatter.41
  1327.6 57.0 reduce-scatter.31
  1389.4 57.1 reduce-scatter.29
  1451.6 64.2 reduce-scatter.39
where the time goes:
time: 1530 us; the launch traced here: 1520 us
  waiting for transfers between devices  949 us (62%)
  matrix products  228 us (15%)
  blocking collectives  143 us (9%)
  other arithmetic  115 us (8%)
  local copies, waits for them, and re-layouts  45.7 us (3%)
  loops' own time  16.1 us (1%)
  between operations  16.1 us (1%)
    unnamed x24, waiting for transfers between devices  144 us
    reduce_scatter x4, waiting for transfers between devices, col_sums(): return lax.psum_scatter(values, 'col', scatter_dimension=0, tiled=True)  139 us
    all_gather x3, waiting for transfers between devices, widen(): return lax.all_gather(values, 'col', axis=0, tiled=True)  100 us
    reduce_scatter x1, waiting for transfers between devices, shards(): lax.psum_scatter(grad_up, 'row', scatter_dimension=0, tiled=True)  94.5 us
    reduce_scatter x1, waiting for transfers between devices, shards(): lax.psum_scatter(grad_gate, 'row', scatter_dimension=0, tiled=True)  94 us
    reduce_scatter x1, waiting for transfers between devices, shards(): lax.psum_scatter(grad_down, 'row', scatter_dimension=1, tiled=True)  89.2 us
    reduce_scatter x1, waiting for transfers between devices, shards(): lax.psum_scatter(grad_key, 'row', scatter_dimension=0, tiled=True)  61.8 us
    reduce_scatter x1, waiting for transfers between devices, shards(): lax.psum_scatter(grad_value, 'row', scatter_dimension=0, tiled=True)  61.6 us
  transfers between devices with their start and end apart: 24, of which 21 were waited for; matrix products, arithmetic and copies ran while one was open for 13% of the time, Pallas kernels for 0%

commit v1 on v0

--- a/solution.py
+++ b/solution.py
@@ -10,6 +10,27 @@
 eps = 1e-05
 rope_base = 10000.0
 neg_fill = -1e30
+
+
+def collect(x, axis, dim):
+    size, place, span = (lax.axis_size(axis), lax.axis_index(axis), x.shape[dim])
+    forward = [(i, (i + 1) % size) for i in range(size)]
+    left = [(i, (i - 1) % size) for i in range(size)]
+    out = jnp.zeros((*x.shape[:dim], size * span, *x.shape[dim + 1 :]), x.dtype)
+    out = lax.dynamic_update_slice_in_dim(out, x, place * span, axis=dim)
+    from_left = from_right = x
+    half = size // 2
+    for step in range(1, half + 1):
+        from_left = lax.ppermute(from_left, axis, forward)
+        out = lax.dynamic_update_slice_in_dim(
+            out, from_left, (place - step) % size * span, axis=dim
+        )
+        if step < size - half:
+            from_right = lax.ppermute(from_right, axis, left)
+            out = lax.dynamic_update_slice_in_dim(
+                out, from_right, (place + step) % size * span, axis=dim
+            )
+    return out
 
 
 def rotate_half(values, head_size):
@@ -93,7 +114,7 @@
         lax.all_gather(key_weight, "row", axis=0, tiled=True),
         lax.all_gather(value_weight, "row", axis=0, tiled=True),
         lax.all_gather(out_weight, "row", axis=1, tiled=True),
-        lax.all_gather(gate_weight, "row", axis=0, tiled=True),
+        collect(gate_weight, "row", 0),
         lax.all_gather(up_weight, "row", axis=0, tiled=True),
         lax.all_gather(down_weight, "row", axis=1, tiled=True),
     )

time: 1530 us -> 1490 us (0.974)
  waiting for transfers between devices: 949 us -> 864 us
  starting transfers between devices: 10.2 us -> 38.1 us
  local copies, waits for them, and re-layouts: 45.7 us -> 62.8 us
    reduce_scatter x4, waiting for transfers between devices: 139 us -> 97.5 us  [col_sums(): return lax.psum_scatter(values, 'col', scatter_dimension=0, tiled=True)]
    all_gather x1 -> x0, waiting for transfers between devices: 40.2 us -> none  [shards(): lax.all_gather(gate_weight, 'row', axis=0, tiled=True)]
    ppermute x0 -> x15, starting transfers between devices: none -> 27.9 us  [the longest x7 27.5 us: collect(): from_right = lax.ppermute(from_right, axis, left)]
    ppermute x0 -> x15, waiting for transfers between devices: none -> 19.8 us  [the longest x8 11.7 us: collect(): from_left = lax.ppermute(from_left, axis, forward)]
    all_gather x3, waiting for transfers between devices: 100 us -> 82.2 us  [widen(): return lax.all_gather(values, 'col', axis=0, tiled=True)]
    unnamed x24 -> x23, waiting for transfers between devices: 144 us -> 143 us
  transfers between devices with their start and end apart: 24 -> 38, of which waited for: 21 -> 27; matrix products, arithmetic and copies ran while one was open for 13% -> 14% of each run, Pallas kernels for 0% -> 0%
where the time goes in v1:
time: 1490 us; the launch traced here: 1480 us
  waiting for transfers between devices  864 us (58%)
  matrix products  229 us (15%)
  blocking collectives  143 us (10%)
  other arithmetic  116 us (8%)
  local copies, waits for them, and re-layouts  62.8 us (4%)
  starting transfers between devices  38.1 us (3%)
  loops' own time  16.1 us (1%)
  between operations  15.9 us (1%)
    unnamed x23, waiting for transfers between devices  143 us
    reduce_scatter x4, waiting for transfers between devices, col_sums(): return lax.psum_scatter(values, 'col', scatter_dimension=0, tiled=True)  97.5 us
    reduce_scatter x1, waiting for transfers between devices, shards(): lax.psum_scatter(grad_gate, 'row', scatter_dimension=0, tiled=True)  94.5 us
    reduce_scatter x1, waiting for transfers between devices, shards(): lax.psum_scatter(grad_up, 'row', scatter_dimension=0, tiled=True)  94.1 us
    reduce_scatter x1, waiting for transfers between devices, shards(): lax.psum_scatter(grad_down, 'row', scatter_dimension=1, tiled=True)  89.2 us
    all_gather x3, waiting for transfers between devices, widen(): return lax.all_gather(values, 'col', axis=0, tiled=True)  82.2 us
    reduce_scatter x1, waiting for transfers between devices, shards(): lax.psum_scatter(grad_value, 'row', scatter_dimension=0, tiled=True)  61.8 us
    reduce_scatter x1, waiting for transfers between devices, shards(): lax.psum_scatter(grad_key, 'row', scatter_dimension=0, tiled=True)  61.6 us
  transfers between devices with their start and end apart: 38, of which 27 were waited for; matrix products, arithmetic and copies ran while one was open for 14% of the time, Pallas kernels for 0%

profile of v1, /device:TPU:0, one launch (start us, length us, event | category | flops | bytes accessed | tf_op | source)
XLA Modules:
  0.0 1484.5 jit_solution(16781749283613685557)
XLA Ops:
  14.6 24.8 %all_gather.39 = bf16[1152,192]{1,0:T(8,128)(2,1)S(1)} all-gather(bf16[72,192]{1,0:T(8,128)(2,1)S(1)} %copy-done.33), channel_id=1, replica_groups=mesh['row'=16,'col'=2] {'row'}, dimensions={0}, use_global_device_ids=true | all-gather | bytes 470016 | tf_op jit(solution)/shard_map/all_gather | solution.py:114
  39.4 19.0 %all_gather.37 = bf16[1152,192]{1,0:T(8,128)(2,1)S(1)} all-gather(bf16[72,192]{1,0:T(8,128)(2,1)S(1)} %copy-done.34), channel_id=1, replica_groups=mesh['row'=16,'col'=2] {'row'}, dimensions={0}, use_global_device_ids=true | all-gather | bytes 470016 | tf_op jit(solution)/shard_map/all_gather | solution.py:115
  62.3 12.0 all_gather.40
  76.3 11.4 all_gather.38
  115.5 11.3 fusion.64
  126.8 62.2 %while.50 = (s32[]{:T(128)}, bf16[6,512,192]{1,2,0:T(8,128)(2,1)S(1)}, f32[6,3,512]{2,1,0:T(4,128)}, s32[6]{0:T(128)S(1)}, bf16[1024,384]{0,1:T(8,128)(2,1)}, /*...) while((s32[]{:T(128)}, ...), condition=%wide.region_6.7_spmd.clone.clone, body=%wide.region_3.6_spmd.clone.sunk.clone | while | flops 418380288 | bytes 22477056 | solution.py:189
  189.0 17.3 %all_to_all.64 = bf16[512,2,576]{0,2,1:T(8,128)(2,1)S(1)} all-to-all(bf16[512,2,576]{0,2,1:T(8,128)(2,1)S(1)} %bitcast.276), channel_id=1, replica_groups=mesh['row'=16,'col'=2] {'col'}, dimensions={1} | all-to-all | bytes 2359296 | tf_op jit(solution)/shard_map/all_to_all | solution.py:74
  256.1 14.7 reduce-scatter.18.cloned.1.call-done
  299.7 8.7 all-gather.21.cloned.1.call-done
  308.4 49.6 %all-gather.19.cloned.1.call-done = bf16[1536,1152]{0,1:T(8,128)(2,1)} async-done(((bf16[1536,72]{0,1:T(8,128)(2,1)}), bf16[1536,1152]{0,1:T(8,128)(2,1)}) %all-gather.19.cloned.1.call-update) | async-done | bytes 3538960 | tf_op jit(solution)/shard_map/all_gather | solution.py:119
  358.0 9.7 fusion.127
  367.7 39.1 %all-gather.17.cloned.1.call-done = bf16[1152,1536]{1,0:T(8,128)(2,1)} async-done(((bf16[72,1536]{1,0:T(8,128)(2,1)}), bf16[1152,1536]{1,0:T(8,128)(2,1)}) %all-gather.17.cloned.1.call-update) | async-done | bytes 3538960 | tf_op jit(solution)/shard_map/all_gather | solution.py:118
  406.8 37.3 %all-gather.15.cloned.1.call-done = bf16[1024,1152]{1,0:T(8,128)(2,1)} async-done(((bf16[512,1152]{1,0:T(8,128)(2,1)}), bf16[1024,1152]{1,0:T(8,128)(2,1)}) %all-gather.15.cloned.1.call-update) | async-done | bytes 2359312 | tf_op jit(solution)/shard_map/all_gather | solution.py:82
  444.1 9.7 fusion.125
  453.8 11.2 multiply_convert_fusion.1
  469.3 8.0 convolution_add_fusion.2
  477.8 59.7 %reduce-scatter.22.cloned.1.call-done = f32[512,1152]{1,0:T(8,128)} async-done(((f32[1024,1152]{1,0:T(8,128)}), f32[512,1152]{1,0:T(8,128)}) %reduce-scatter.22.cloned.1.call-update) | async-done | bytes 2359312 | tf_op jit(solution)/shard_map/reduce_scatter | solution.py:78
  543.5 36.2 %all-gather.23.cloned.1.call-done = bf16[1024,1152]{1,0:T(8,128)(2,1)} async-done(((bf16[512,1152]{1,0:T(8,128)(2,1)}), bf16[1024,1152]{1,0:T(8,128)(2,1)}) %all-gather.23.cloned.1.call-update) | async-done | bytes 2359312 | tf_op jit(solution)/shard_map/all_gather | solution.py:82
  589.1 15.3 %all-to-all-done.2 = bf16[2,512,576]{1,2,0:T(8,128)(2,1)} async-done(((bf16[2,512,576]{1,2,0:T(8,128)(2,1)}), bf16[2,512,576]{1,2,0:T(8,128)(2,1)}, u32[]{:S(2)}, u32[]{:S(2)}) %all-to-all-start.2) | async-done | bytes 1179680 | tf_op jit(solution)/shard_map/all_to_all | solution.py:70
  607.2 125.1 %while.51 = (s32[]{:T(128)}, f32[1024,384]{0,1:T(8,128)}, f32[1024,384]{0,1:T(8,128)}, f32[6,512,192]{1,2,0:T(8,128)}, s32[6]{0:T(128)S(1)}, /*index=5*/bf16[102...) while((s32[]{:T(128)}, f32[1024,384]{0,1:T(8,128)}, ...), condition=%wide.region_15.16_spmd.clone.clone, body=%wide.region_13.15_spmd.clone.sunk.clone | while | flops 1027209728 | bytes 55630144 | solution.py:286
  758.4 8.7 subtract_convert_fusion
  767.1 18.8 %all_to_all.65 = bf16[512,2,576]{0,2,1:T(8,128)(2,1)S(1)} all-to-all(bf16[512,2,576]{0,2,1:T(8,128)(2,1)S(1)} %subtract_convert_fusion), channel_id=1, replica_groups=mesh['row'=16,'col'=2] {'col'}, dimensions={1} | all-to-all | bytes 2359296 | tf_op jit(solution)/shard_map/all_to_all | solution.py:74
  808.6 9.4 fusion.126
  871.6 40.1 %all-reduce.2 = (f32[1152]{0:T(1024)}, f32[1152]{0:T(1024)}) all-reduce(f32[1152]{0:T(1024)} %get-tuple-element.251, f32[1152]{0:T(1024)} %get-tuple-element.249), channel_id=1, replica_groups=mesh['row'=16,'col'=2] {'row','col'}, use_global_device_ids=true, to_apply=%region_21.22 | all-reduce | flops 2304 | bytes 18432 | tf_op jit(solution)/shard_map/psum | solution.py:343
  913.0 19.2 %reduce-scatter.20.cloned.1.call-done = f32[512,1152]{1,0:T(8,128)} async-done(((f32[1024,1152]{1,0:T(8,128)}), f32[512,1152]{1,0:T(8,128)}) %reduce-scatter.20.cloned.1.call-update) | async-done | bytes 2359312 | tf_op jit(solution)/shard_map/reduce_scatter | solution.py:78
  937.3 89.2 %reduce-scatter.38.cloned.1.call-done = f32[1536,72]{0,1:T(8,128)} async-done(((f32[1536,1152]{0,1:T(8,128)}), f32[1536,72]{0,1:T(8,128)}) %reduce-scatter.38.cloned.1.call-update) | async-done | bytes 442384 | tf_op jit(solution)/shard_map/reduce_scatter | solution.py:341
  1026.5 94.5 %reduce-scatter.34.cloned.1.call-done = f32[72,1536]{1,0:T(8,128)} async-done(((f32[1152,1536]{1,0:T(8,128)}), f32[72,1536]{1,0:T(8,128)}) %reduce-scatter.34.cloned.1.call-update) | async-done | bytes 442384 | tf_op jit(solution)/shard_map/reduce_scatter | solution.py:339
  1121.0 94.1 %reduce-scatter.36.cloned.1.call-done = f32[72,1536]{1,0:T(8,128)} async-done(((f32[1152,1536]{1,0:T(8,128)}), f32[72,1536]{1,0:T(8,128)}) %reduce-scatter.36.cloned.1.call-update) | async-done | bytes 442384 | tf_op jit(solution)/shard_map/reduce_scatter | solution.py:340
  1215.2 69.6 %reduce-scatter.42.cloned.1.call-done = f32[576,72]{0,1:T(8,128)} async-done(((f32[576,1152]{0,1:T(8,128)}), f32[576,72]{0,1:T(8,128)}) %reduce-scatter.42.cloned.1.call-update) | async-done | bytes 165904
  1284.8 61.8 %reduce-scatter.32.cloned.1.call-done = f32[72,192]{1,0:T(8,128)} async-done(((f32[1152,192]{1,0:T(8,128)}), f32[72,192]{1,0:T(8,128)}) %reduce-scatter.32.cloned.1.call-update) | async-done | bytes 55312 | tf_op jit(solution)/shard_map/reduce_scatter | solution.py:337
  1346.6 61.6 %reduce-scatter.30.cloned.1.call-done = f32[72,192]{1,0:T(8,128)} async-done(((f32[1152,192]{1,0:T(8,128)}), f32[72,192]{1,0:T(8,128)}) %reduce-scatter.30.cloned.1.call-update) | async-done | bytes 55312 | tf_op jit(solution)/shard_map/reduce_scatter | solution.py:336
  1408.2 69.3 %reduce-scatter.40.cloned.1.call-done = f32[72,576]{1,0:T(8,128)} async-done(((f32[1152,576]{1,0:T(8,128)}), f32[72,576]{1,0:T(8,128)}) %reduce-scatter.40.cloned.1.call-update) | async-done | bytes 165904
  (404 shorter events, 421.0 us)
Async XLA Ops:
  7.2 51.2 %all-gather.9.cloned.1.call-start = ((), (), s32[]{:S(2)}) async-start(), calls=%async_computation.17 | async-start | bytes 3538944 | tf_op jit(solution)/shard_map/all_gather | solution.py:110
  8.0 82.0 %all-gather.11.cloned.1.call-start = ((), (), s32[]{:S(2)}) async-start(), calls=%async_computation.18 | async-start | bytes 1566720 | tf_op jit(solution)/shard_map/all_gather | solution.py:113
  8.7 197.8 %all-gather.13.cloned.1.call-start = ((), (), s32[]{:S(2)}) async-start(), calls=%async_computation.19 | async-start | bytes 1566720 | tf_op jit(solution)/shard_map/all_gather | solution.py:116
  95.1 19.3 %all-to-all-start = ((bf16[2,512,576]{1,2,0:T(8,128)(2,1)}), bf16[2,512,576]{1,2,0:T(8,128)(2,1)S(1)}, u32[]{:S(2)}, u32[]{:S(2)}) async-start(bf16[2,512,576]{1,2,0:T(8,128)(2,1)} %bitcast.277), calls=%async_computation | async-start | bytes 2359296 | tf_op jit(solution)/shard_map/all_to_all | solution.py:70
  98.7 172.1 %reduce-scatter.18.cloned.1.call-start = ((), (), s32[]{:S(2)}) async-start(), calls=%async_computation.20 | async-start | bytes 7077888 | tf_op jit(solution)/shard_map/reduce_scatter | solution.py:78
  212.8 95.6 %all-gather.21.cloned.1.call-start = ((), (), s32[]{:S(2)}) async-start(), calls=%async_computation.25 | async-start | bytes 3538944 | tf_op jit(solution)/shard_map/all_gather | solution.py:82
  213.3 144.7 %all-gather.19.cloned.1.call-start = ((), (), s32[]{:S(2)}) async-start(), calls=%async_computation.23 | async-start | bytes 3760128 | tf_op jit(solution)/shard_map/all_gather | solution.py:119
  213.9 192.9 %all-gather.17.cloned.1.call-start = ((), (), s32[]{:S(2)}) async-start(), calls=%async_computation.22 | async-start | bytes 3760128 | tf_op jit(solution)/shard_map/all_gather | solution.py:118
  214.7 229.4 %all-gather.15.cloned.1.call-start = ((), (), s32[]{:S(2)}) async-start(), calls=%async_computation.21 | async-start | bytes 3538944 | tf_op jit(solution)/shard_map/all_gather | solution.py:82
  215.0 8.2 collective-permute-start
  223.2 8.2 collective-permute-start.2
  226.6 8.2 collective-permute-start.5
  231.4 8.2 collective-permute-start.4
  247.7 8.3 collective-permute-start.8
  251.1 27.9 %collective-permute-start.11 = (bf16[72,1536]{1,0:T(8,128)(2,1)}, bf16[72,1536]{1,0:T(8,128)(2,1)}, u32[]{:S(2)}, u32[]{:S(2)}) collective-permute-start(bf16[72,1536]{1,0:T(8,128)(2,1)} %collective-permute-done.9), channel_id=1, source_target_pairs={{0,30},{2,0},{4,2},{6,4},{8,6},{10,8},{12,10},{14,12},{16,14},{18,... | collective-permute-start | bytes 663560 | tf_op jit(solution)/shard_map/ppermute | solution.py:29
  256.0 26.7 %collective-permute-start.10 = (bf16[72,1536]{1,0:T(8,128)(2,1)}, bf16[72,1536]{1,0:T(8,128)(2,1)}, u32[]{:S(2)}, u32[]{:S(2)}) collective-permute-start(bf16[72,1536]{1,0:T(8,128)(2,1)} %collective-permute-done.8), channel_id=1, source_target_pairs={{0,2},{2,4},{4,6},{6,8},{8,10},{10,12},{12,14},{14,16},{16,18},{18... | collective-permute-start | bytes 663560 | tf_op jit(solution)/shard_map/ppermute | solution.py:24
  275.7 261.8 %reduce-scatter.22.cloned.1.call-start = ((), (), s32[]{:S(2)}) async-start(), calls=%async_computation.26 | async-start | bytes 7077888 | tf_op jit(solution)/shard_map/reduce_scatter | solution.py:78
  279.0 12.6 collective-permute-start.13
  282.7 8.3 collective-permute-start.12
  477.4 102.3 %all-gather.23.cloned.1.call-start = ((), (), s32[]{:S(2)}) async-start(), calls=%async_computation.27 | async-start | bytes 3538944 | tf_op jit(solution)/shard_map/all_gather | solution.py:82
  584.6 19.8 %all-to-all-start.2 = ((bf16[2,512,576]{1,2,0:T(8,128)(2,1)}), bf16[2,512,576]{1,2,0:T(8,128)(2,1)}, u32[]{:S(2)}, u32[]{:S(2)}) async-start(bf16[2,512,576]{1,2,0:T(8,128)(2,1)} %bitcast.162), calls=%async_computation.5 | async-start | bytes 2359296 | tf_op jit(solution)/shard_map/all_to_all | solution.py:70
  589.1 201.4 %reduce-scatter.24.cloned.1.call-start = ((), (), s32[]{:S(2)}) async-start(), calls=%async_computation.28 | async-start | bytes 2359296 | tf_op jit(solution)/shard_map/reduce_scatter | solution.py:308
  747.1 55.7 %reduce-scatter.26.cloned.1.call-start = ((), (), s32[]{:S(2)}) async-start(), calls=%async_computation.29 | async-start | bytes 2359296 | tf_op jit(solution)/shard_map/reduce_scatter | solution.py:309
  756.1 112.6 %reduce-scatter.28.cloned.1.call-start = ((), (), s32[]{:S(2)}) async-start(), calls=%async_computation.30 | async-start | bytes 7077888 | tf_op jit(solution)/shard_map/reduce_scatter | solution.py:78
  808.5 123.7 %reduce-scatter.20.cloned.1.call-start = ((), (), s32[]{:S(2)}) async-start(), calls=%async_computation.24 | async-start | bytes 7077888 | tf_op jit(solution)/shard_map/reduce_scatter | solution.py:78
  818.0 208.5 %reduce-scatter.38.cloned.1.call-start = ((), (), s32[]{:S(2)}) async-start(), calls=%async_computation.35 | async-start | bytes 7520256 | tf_op jit(solution)/shard_map/reduce_scatter | solution.py:341
  827.3 293.7 %reduce-scatter.34.cloned.1.call-start = ((), (), s32[]{:S(2)}) async-start(), calls=%async_computation.33 | async-start | bytes 7520256 | tf_op jit(solution)/shard_map/reduce_scatter | solution.py:339
  836.5 378.6 %reduce-scatter.36.cloned.1.call-start = ((), (), s32[]{:S(2)}) async-start(), calls=%async_computation.34 | async-start | bytes 7520256 | tf_op jit(solution)/shard_map/reduce_scatter | solution.py:340
  844.5 440.3 %reduce-scatter.42.cloned.1.call-start = ((), (), s32[]{:S(2)}) async-start(), calls=%async_computation.37 | async-start | bytes 3133440
  851.1 495.5 %reduce-scatter.32.cloned.1.call-start = ((), (), s32[]{:S(2)}) async-start(), calls=%async_computation.32 | async-start | bytes 1253376 | tf_op jit(solution)/shard_map/reduce_scatter | solution.py:337
  855.9 552.3 %reduce-scatter.30.cloned.1.call-start = ((), (), s32[]{:S(2)}) async-start(), calls=%async_computation.31 | async-start | bytes 1253376 | tf_op jit(solution)/shard_map/reduce_scatter | solution.py:336
  859.2 618.2 %reduce-scatter.40.cloned.1.call-start = ((), (), s32[]{:S(2)}) async-start(), calls=%async_computation.36 | async-start | bytes 3133440
  (66 other events, 1205.8 us)
Sparse Core Ops, SparseCore 0:
  9.6 38.7 all-gather.8
  50.6 39.3 all-gather.10
  92.1 38.1 all-gather.12
  212.9 57.8 reduce-scatter.17
  272.3 36.0 all-gather.20
  310.8 47.1 all-gather.18
  360.6 46.1 all-gather.16
  409.0 35.0 all-gather.14
  477.5 59.9 reduce-scatter.21
  543.6 36.0 all-gather.22
  747.2 26.4 reduce-scatter.23
  775.8 26.8 reduce-scatter.25
  808.6 59.9 reduce-scatter.27
  870.9 61.2 reduce-scatter.19
  936.6 89.8 reduce-scatter.37
  1031.5 89.4 reduce-scatter.33
  1125.5 89.6 reduce-scatter.35
  1220.0 64.7 reduce-scatter.41
  1289.4 57.1 reduce-scatter.31
  1351.0 57.0 reduce-scatter.29
  1413.2 64.2 reduce-scatter.39
